TPU v7x, 256 devices: a whole 4x4x8 slice. The times are simulated.
256 devices in a mesh: layer: 8 (over x, core), feat: 32 (over y, z).
Axes of the slice: x: 4, y: 4, z: 8, core: 2. Of those that a mesh axis runs over, the one named last changes fastest.
Arguments:
- gradient: bfloat16 [8, 2560, 2560], P('layer', 'feat'), may hold values from -3 to 3
- in_inverse: bfloat16 [8, 2560, 2560], P('layer', 'feat'), may hold values from -1 to 2.5, as said below
- in_coupling: bfloat16 [8, 2560, 2560], P('layer', 'feat'), may hold values from -0.125 to 0.125
- in_carry: bfloat16 [8, 2560, 2560], P('layer', 'feat'), may hold values from -0.125 to 0.125
- out_inverse: bfloat16 [8, 20, 128, 128], P('layer'), may hold values from -1 to 2.5, as said below
- out_coupling: bfloat16 [8, 20, 128, 128], P('layer'), may hold values from -0.5 to 0.5
Outputs:
- update: bfloat16 [8, 2560, 2560], P('layer', 'feat')
Inputs may be any that keep to these rules, and one draw needn't show every extreme that they name: `in_inverse`: symmetric in its last two dimensions. `out_inverse`: symmetric in its last two dimensions.
All inputs are finite; a program needn't handle non-finite values.
Results may differ from a plain program's by a relative error of at most 0.006.
Values may be sent and summed in bfloat16 or wider, within the bound.
No kernel may reach another device: no remote copies, remote signals or barrier semaphores. Data moves between devices by JAX's collectives and lax.ppermute only.
A program may use at most 64 MiB of HBM per device.

v0:
```python
import jax
import jax.numpy as jnp
from jax import lax
from jax.sharding import PartitionSpec as P


def from_behind(x, axis, by):
    size = lax.axis_size(axis)
    pairs = [(i, i + by) for i in range(size) if 0 <= i + by < size]
    return lax.ppermute(x, axis, pairs)


def block_apply(matrix, table, flipped):
    row_count = matrix.shape[0]
    blocks = table.shape[0]
    block_width = table.shape[1]
    grouped = matrix.reshape(row_count, blocks, block_width)
    pattern = "rnb,ncb->rnc" if flipped else "rnb,nbc->rnc"
    product = jnp.einsum(pattern, grouped, table, preferred_element_type=jnp.float32)
    return product.reshape(row_count, blocks * block_width)


def contract_rows(factor, piece):
    return jnp.dot(factor, piece, preferred_element_type=jnp.float32)


def local(gradient, in_inverse, in_coupling, in_carry, out_inverse, out_coupling):
    grad_rows = gradient[0]
    inverse_rows = in_inverse[0]
    coupling_rows = in_coupling[0]
    carry_rows = in_carry[0]
    out_inv = out_inverse[0]
    out_psi = out_coupling[0]
    psi_from_below = from_behind(out_psi, "layer", 1)
    from_above = from_behind(grad_rows, "layer", -1)
    near_rows = block_apply(from_above, out_psi, True).astype(jnp.bfloat16)
    coupled = contract_rows(coupling_rows, lax.all_gather(near_rows, "feat", axis=0, tiled=True))
    reduced = (grad_rows.astype(jnp.float32) - coupled).astype(jnp.bfloat16)
    piece = lax.all_gather(reduced, "feat", axis=0, tiled=True)
    whitened_acc = contract_rows(inverse_rows, piece)
    carried_acc = contract_rows(carry_rows, piece)
    whitened = whitened_acc.astype(jnp.bfloat16)
    carried = carried_acc.astype(jnp.bfloat16)
    local_term = block_apply(whitened, out_inv, False)
    middle = block_apply(carried, out_inv, False).astype(jnp.bfloat16)
    middle_from_below = from_behind(middle, "layer", 1)
    incoming = block_apply(middle_from_below, psi_from_below, False)
    return (local_term - incoming).astype(jnp.bfloat16)[None]


def solution(mesh):
    return jax.shard_map(
        local,
        mesh=mesh,
        in_specs=(
            P("layer", "feat", None),
            P("layer", "feat", None),
            P("layer", "feat", None),
            P("layer", "feat", None),
            P("layer", None, None, None),
            P("layer", None, None, None),
        ),
        out_specs=P("layer", "feat", None),
        check_vma=False,
    )
```

profile of v0, /device:TPU:1, one launch (start us, length us, event | category | flops | bytes accessed | tf_op | source)
XLA Modules:
  0.0 296.4 jit_solution(8207980276232798761)
XLA Ops:
  6.5 0.0 all-gather.3.cloned.1.call-start
  6.5 5.3 %collective-permute-start = (bf16[80,2560]{1,0:T(8,128)(2,1)}, bf16[80,2560]{1,0:T(8,128)(2,1)S(1)}, u32[]{:S(2)}, u32[]{:S(2)}) collective-permute-start(bf16[80,2560]{1,0:T(8,128)(2,1)} %bitcast.72), channel_id=1, source_target_pairs={{32,0},{64,32},{96,64},{128,96},{160,128},{192,160},{224,192},{33,... | collective-permute-start | bytes 1228808 | tf_op jit(solution)/shard_map/ppermute | solution.py:10
  11.8 5.2 %collective-permute-done = bf16[80,2560]{1,0:T(8,128)(2,1)S(1)} collective-permute-done((bf16[80,2560]{1,0:T(8,128)(2,1)}, bf16[80,2560]{1,0:T(8,128)(2,1)S(1)}, u32[]{:S(2)}, u32[]{:S(2)}) %collective-permute-start) | collective-permute-done | bytes 409632 | tf_op jit(solution)/shard_map/ppermute | solution.py:10
  17.0 1.7 fusion.6
  18.7 0.8 copy.41
  19.5 0.0 all-gather.3.cloned.1.call-update
  19.5 0.0 all-gather.5.cloned.1.call-start
  19.6 124.4 %all-gather.3.cloned.1.call-done = bf16[2560,2560]{1,0:T(8,128)(2,1)} async-done(((bf16[80,2560]{1,0:T(8,128)(2,1)}), bf16[2560,2560]{1,0:T(8,128)(2,1)}) %all-gather.3.cloned.1.call-update) | async-done | bytes 13107216 | tf_op jit(solution)/shard_map/all_gather | solution.py:37
  144.0 8.0 %fusion.1 = bf16[80,2560]{1,0:T(8,128)(2,1)} fusion(bf16[2560,2560]{1,0:T(8,128)(2,1)} %all-gather.3.cloned.1.call-done, bf16[1,80,2560]{2,1,0:T(8,128)(2,1)} %param.8, bf16[1,80,2560]{2,1,0:T(8,128)(2,1)} %param.6), kind=kOutput, calls=%fused_computation.2 | convolution fusion | flops 1049190400 | bytes 14336000 | tf_op jit(solution)/shard_map/dot_general | solution.py:24
  152.0 0.0 all-gather.5.cloned.1.call-update
  152.0 4.2 %collective-permute-start.2 = (bf16[20,128,128]{2,1,0:T(8,128)(2,1)S(1)}, bf16[20,128,128]{2,1,0:T(8,128)(2,1)S(1)}, u32[]{:S(2)}, u32[]{:S(2)}) collective-permute-start(bf16[20,128,128]{2,1,0:T(8,128)(2,1)S(1)} %bitcast.70), channel_id=1, source_target_pairs={{0,32},{32,64},{64,96},{96,128},{128,160},{160,192},{192,224},{1,3... | collective-permute-start | bytes 1966088 | tf_op jit(solution)/shard_map/ppermute | solution.py:10
  156.2 115.3 %all-gather.5.cloned.1.call-done = bf16[2560,2560]{1,0:T(8,128)(2,1)} async-done(((bf16[80,2560]{1,0:T(8,128)(2,1)}), bf16[2560,2560]{1,0:T(8,128)(2,1)}) %all-gather.5.cloned.1.call-update) | async-done | bytes 13107216 | tf_op jit(solution)/shard_map/all_gather | solution.py:39
  271.5 0.0 copy-done.2
  271.5 7.3 %fusion.4 = bf16[10,20,8,128]{3,2,1,0:T(8,128)(2,1)S(1)} fusion(bf16[2560,2560]{1,0:T(8,128)(2,1)} %all-gather.5.cloned.1.call-done, bf16[1,80,2560]{2,1,0:T(8,128)(2,1)S(1)} %copy-done.2), kind=kOutput, calls=%fused_computation.10 | convolution fusion | flops 1048780800 | bytes 13926400 | tf_op jit(solution)/shard_map/dot_general | solution.py:24
  278.7 0.4 fusion.7
  279.1 0.1 copy.40
  279.2 4.0 %collective-permute-start.1 = (bf16[80,2560]{1,0:T(8,128)(2,1)S(1)}, bf16[80,2560]{1,0:T(8,128)(2,1)S(1)}, u32[]{:S(2)}, u32[]{:S(2)}) collective-permute-start(bf16[80,2560]{1,0:T(8,128)(2,1)S(1)} %bitcast.71), channel_id=1, source_target_pairs={{0,32},{32,64},{64,96},{96,128},{128,160},{160,192},{192,224},{1,3... | collective-permute-start | bytes 1228808 | tf_op jit(solution)/shard_map/ppermute | solution.py:10
  283.2 2.4 fusion.3
  285.6 0.4 fusion.9
  286.0 0.0 collective-permute-done.2
  286.0 2.1 collective-permute-done.1
  288.1 0.4 fusion.5
  288.5 0.1 copy.15
  288.6 1.0 convert_element_type.66
  (9 shorter events, 0.0 us)
Async XLA Ops:
  6.5 272.2 %copy-start = (bf16[1,20,128,128]{3,2,1,0:T(8,128)(2,1)S(1)}, bf16[1,20,128,128]{3,2,1,0:T(8,128)(2,1)}, u32[]{:S(2)}) copy-start(bf16[1,20,128,128]{3,2,1,0:T(8,128)(2,1)} %param.10) | copy-start | bytes 1966084
  6.5 145.5 %copy-start.4 = (bf16[1,20,128,128]{3,2,1,0:T(8,128)(2,1)S(1)}, bf16[1,20,128,128]{3,2,1,0:T(8,128)(2,1)}, u32[]{:S(2)}) copy-start(bf16[1,20,128,128]{3,2,1,0:T(8,128)(2,1)} %param.11) | copy-start | bytes 1966084
  6.5 264.9 %copy-start.2 = (bf16[1,80,2560]{2,1,0:T(8,128)(2,1)S(1)}, bf16[1,80,2560]{2,1,0:T(8,128)(2,1)}, u32[]{:S(2)}) copy-start(bf16[1,80,2560]{2,1,0:T(8,128)(2,1)} %param.9) | copy-start | bytes 1228804
  6.5 137.4 %all-gather.3.cloned.1.call-start = ((), (), s32[]{:S(2)}) async-start(), calls=%async_computation | async-start | bytes 13516800 | tf_op jit(solution)/shard_map/all_gather | solution.py:37
  6.5 10.5 %collective-permute-start = (bf16[80,2560]{1,0:T(8,128)(2,1)}, bf16[80,2560]{1,0:T(8,128)(2,1)S(1)}, u32[]{:S(2)}, u32[]{:S(2)}) collective-permute-start(bf16[80,2560]{1,0:T(8,128)(2,1)} %bitcast.72), channel_id=1, source_target_pairs={{32,0},{64,32},{96,64},{128,96},{160,128},{192,160},{224,192},{33,... | collective-permute-start | bytes 1228808 | tf_op jit(solution)/shard_map/ppermute | solution.py:10
  19.5 251.9 %all-gather.5.cloned.1.call-start = ((), (), s32[]{:S(2)}) async-start(), calls=%async_computation.1 | async-start | bytes 13516800 | tf_op jit(solution)/shard_map/all_gather | solution.py:39
  152.0 131.2 %copy-start.3 = (bf16[1,80,2560]{2,1,0:T(8,128)(2,1)S(1)}, bf16[1,80,2560]{2,1,0:T(8,128)(2,1)}, u32[]{:S(2)}) copy-start(bf16[1,80,2560]{2,1,0:T(8,128)(2,1)} %param.7) | copy-start | bytes 1228804
  152.0 134.0 %collective-permute-start.2 = (bf16[20,128,128]{2,1,0:T(8,128)(2,1)S(1)}, bf16[20,128,128]{2,1,0:T(8,128)(2,1)S(1)}, u32[]{:S(2)}, u32[]{:S(2)}) collective-permute-start(bf16[20,128,128]{2,1,0:T(8,128)(2,1)S(1)} %bitcast.70), channel_id=1, source_target_pairs={{0,32},{32,64},{64,96},{96,128},{128,160},{160,192},{192,224},{1,3... | collective-permute-start | bytes 1966088 | tf_op jit(solution)/shard_map/ppermute | solution.py:10
  271.5 11.8 %copy-start.1 = (bf16[2560,2560]{1,0:T(8,128)(2,1)S(1)}, bf16[2560,2560]{1,0:T(8,128)(2,1)}, u32[]{:S(2)}) copy-start(bf16[2560,2560]{1,0:T(8,128)(2,1)} %all-gather.5.cloned.1.call-done) | copy-start | bytes 39321604
  279.2 8.9 %collective-permute-start.1 = (bf16[80,2560]{1,0:T(8,128)(2,1)S(1)}, bf16[80,2560]{1,0:T(8,128)(2,1)S(1)}, u32[]{:S(2)}, u32[]{:S(2)}) collective-permute-start(bf16[80,2560]{1,0:T(8,128)(2,1)S(1)} %bitcast.71), channel_id=1, source_target_pairs={{0,32},{32,64},{64,96},{96,128},{128,160},{160,192},{192,224},{1,3... | collective-permute-start | bytes 1228808 | tf_op jit(solution)/shard_map/ppermute | solution.py:10
Sparse Core Ops, SparseCore 0:
  19.7 124.2 all-gather.2
  152.1 119.3 all-gather.4
where the time goes:
time: 297 us; the launch traced here: 296 us
  waiting for transfers between devices  247 us (83%)
  matrix products  20.4 us (7%)
  starting transfers between devices  13.5 us (5%)
  between operations  13.5 us (5%)
    all_gather x1, waiting for transfers between devices, local(): lax.all_gather(near_rows, 'feat', axis=0, tiled=True)  124 us
    all_gather x1, waiting for transfers between devices, local(): piece = lax.all_gather(reduced, 'feat', axis=0, tiled=True)  115 us
    dot_general x3, matrix products, contract_rows(): return jnp.dot(factor, piece, preferred_element_type=jnp.float32)  17.6 us
    ppermute x3, starting transfers between devices, from_behind(): return lax.ppermute(x, axis, pairs)  13.5 us
    ppermute x3, waiting for transfers between devices, from_behind(): return lax.ppermute(x, axis, pairs)  7.29 us
  transfers between devices with their start and end apart: 5, of which 4 were waited for; matrix products, arithmetic and copies ran while one was open for 4% of the time, Pallas kernels for 0%

commit v1 on v0

--- a/solution.py
+++ b/solution.py
@@ -34,7 +34,12 @@
     psi_from_below = from_behind(out_psi, "layer", 1)
     from_above = from_behind(grad_rows, "layer", -1)
     near_rows = block_apply(from_above, out_psi, True).astype(jnp.bfloat16)
-    coupled = contract_rows(coupling_rows, lax.all_gather(near_rows, "feat", axis=0, tiled=True))
+    coupled = contract_rows(
+        coupling_rows,
+        jnp.concatenate(
+            lax.all_to_all(jnp.stack([near_rows] * lax.axis_size("feat")), "feat", 0, 0), axis=0
+        ),
+    )
     reduced = (grad_rows.astype(jnp.float32) - coupled).astype(jnp.bfloat16)
     piece = lax.all_gather(reduced, "feat", axis=0, tiled=True)
     whitened_acc = contract_rows(inverse_rows, piece)

time: 297 us -> 470 us (1.58)
  blocking collectives: 0 us -> 294 us
  waiting for transfers between devices: 247 us -> 123 us
  local copies, waits for them, and re-layouts: 2.04 us -> 7.45 us
  matrix products: 20.4 us -> 15.5 us
    all_to_all x0 -> x1, blocking collectives: none -> 294 us  [local(): lax.all_to_all(jnp.stack([near_rows] * lax.axis_size('feat')), 'feat', 0, 0)]
    all_gather x1 -> x0, waiting for transfers between devices: 124 us -> none  [local(): lax.all_gather(near_rows, 'feat', axis=0, tiled=True)]
    another operation x0 -> x1, local copies, waits for them, and re-layouts: none -> 6.16 us  [local(): jnp.stack([near_rows] * lax.axis_size('feat'))]
    dot_general x3, matrix products: 17.6 us -> 12.8 us  [contract_rows(): return jnp.dot(factor, piece, preferred_element_type=jnp.float32)]
  transfers between devices with their start and end apart: 5 -> 4, of which waited for: 4 -> 3; matrix products, arithmetic and copies ran while one was open for 4% -> 2% of each run, Pallas kernels for 0% -> 0%
where the time goes in v1:
time: 470 us
  blocking collectives  294 us (63%)
  waiting for transfers between devices  123 us (26%)
  starting transfers between devices  16.2 us (3%)
  matrix products  15.5 us (3%)
  between operations  13.5 us (3%)
  local copies, waits for them, and re-layouts  7.45 us (2%)
    all_to_all x1, blocking collectives, local(): lax.all_to_all(jnp.stack([near_rows] * lax.axis_size('feat')), 'feat', 0, 0)  294 us
    all_gather x1, waiting for transfers between devices, local(): piece = lax.all_gather(reduced, 'feat', axis=0, tiled=True)  116 us
    ppermute x3, starting transfers between devices, from_behind(): return lax.ppermute(x, axis, pairs)  16.2 us
    dot_general x3, matrix products, contract_rows(): return jnp.dot(factor, piece, preferred_element_type=jnp.float32)  12.8 us
  transfers between devices with their start and end apart: 4, of which 3 were waited for; matrix products, arithmetic and copies ran while one was open for 2% of the time, Pallas kernels for 0%

profile of v1, /device:TPU:1, one launch (start us, length us, event | category | flops | bytes accessed | tf_op | source)
XLA Modules:
  0.0 469.9 jit_solution(1412267083530222147)
XLA Ops:
  6.5 0.0 copy-start
  6.5 0.0 all-gather.2.cloned.1.call-start
  6.5 5.3 %collective-permute-start = (bf16[80,2560]{1,0:T(8,128)(2,1)}, bf16[80,2560]{1,0:T(8,128)(2,1)S(1)}, u32[]{:S(2)}, u32[]{:S(2)}) collective-permute-start(bf16[80,2560]{1,0:T(8,128)(2,1)} %bitcast.74), channel_id=1, source_target_pairs={{32,0},{64,32},{96,64},{128,96},{160,128},{192,160},{224,192},{33,... | collective-permute-start | bytes 1228808 | tf_op jit(solution)/shard_map/ppermute | solution.py:10
  11.8 5.2 %collective-permute-done = bf16[80,2560]{1,0:T(8,128)(2,1)S(1)} collective-permute-done((bf16[80,2560]{1,0:T(8,128)(2,1)}, bf16[80,2560]{1,0:T(8,128)(2,1)S(1)}, u32[]{:S(2)}, u32[]{:S(2)}) %collective-permute-start) | collective-permute-done | bytes 409632 | tf_op jit(solution)/shard_map/ppermute | solution.py:10
  17.0 1.7 fusion.6
  18.7 0.1 copy.41
  18.8 6.2 %stack.2 = bf16[32,80,2560]{2,1,0:T(8,128)(2,1)} broadcast(bf16[80,2560]{1,0:T(8,128)(2,1)S(1)} %bitcast.71), dimensions={1,2} | broadcast | bytes 13516800 | tf_op jit(solution)/shard_map/stack | solution.py:40
  24.9 293.7 %all_to_all.5 = bf16[32,80,2560]{2,1,0:T(8,128)(2,1)S(1)} all-to-all(bf16[32,80,2560]{2,1,0:T(8,128)(2,1)} %stack.2), channel_id=1, replica_groups=mesh['layer'=8,'feat'=32] {'feat'}, dimensions={0} | all-to-all | bytes 26214400 | tf_op jit(solution)/shard_map/all_to_all | solution.py:40
  318.6 3.1 fusion.1
  321.8 0.0 all-gather.2.cloned.1.call-update
  321.8 0.0 copy-done.5
  321.8 6.9 %collective-permute-start.2 = (bf16[20,128,128]{2,1,0:T(8,128)(2,1)S(1)}, bf16[20,128,128]{2,1,0:T(8,128)(2,1)S(1)}, u32[]{:S(2)}, u32[]{:S(2)}) collective-permute-start(bf16[20,128,128]{2,1,0:T(8,128)(2,1)S(1)} %bitcast.72), channel_id=1, source_target_pairs={{0,32},{32,64},{64,96},{96,128},{128,160},{160,192},{192,224},{1,3... | collective-permute-start | bytes 1966088 | tf_op jit(solution)/shard_map/ppermute | solution.py:10
  328.7 116.2 %all-gather.2.cloned.1.call-done = bf16[2560,2560]{1,0:T(8,128)(2,1)} async-done(((bf16[80,2560]{1,0:T(8,128)(2,1)}), bf16[2560,2560]{1,0:T(8,128)(2,1)}) %all-gather.2.cloned.1.call-update) | async-done | bytes 13107216 | tf_op jit(solution)/shard_map/all_gather | solution.py:44
  444.9 7.3 %fusion.4 = bf16[10,20,8,128]{3,2,1,0:T(8,128)(2,1)S(1)} fusion(bf16[2560,2560]{1,0:T(8,128)(2,1)} %all-gather.2.cloned.1.call-done, bf16[1,80,2560]{2,1,0:T(8,128)(2,1)S(1)} %copy-done.2), kind=kOutput, calls=%fused_computation.10 | convolution fusion | flops 1048780800 | bytes 13926400 | tf_op jit(solution)/shard_map/dot_general | solution.py:24
  452.2 0.4 fusion.7
  452.5 0.1 copy.40
  452.6 4.0 collective-permute-start.1
  456.7 2.4 fusion.3
  459.0 0.4 fusion.9
  459.4 0.0 collective-permute-done.2
  459.4 2.1 collective-permute-done.1
  461.5 0.4 fusion.5
  461.9 0.1 copy.15
  462.0 1.0 convert_element_type.68
  (12 shorter events, 0.0 us)
Async XLA Ops:
  6.5 445.6 %copy-start = (bf16[1,20,128,128]{3,2,1,0:T(8,128)(2,1)S(1)}, bf16[1,20,128,128]{3,2,1,0:T(8,128)(2,1)}, u32[]{:S(2)}) copy-start(bf16[1,20,128,128]{3,2,1,0:T(8,128)(2,1)} %param.10) | copy-start | bytes 1966084
  6.5 438.4 %all-gather.2.cloned.1.call-start = ((), (), s32[]{:S(2)}) async-start(), calls=%async_computation.1 | async-start | bytes 13516800 | tf_op jit(solution)/shard_map/all_gather | solution.py:44
  6.5 10.5 %collective-permute-start = (bf16[80,2560]{1,0:T(8,128)(2,1)}, bf16[80,2560]{1,0:T(8,128)(2,1)S(1)}, u32[]{:S(2)}, u32[]{:S(2)}) collective-permute-start(bf16[80,2560]{1,0:T(8,128)(2,1)} %bitcast.74), channel_id=1, source_target_pairs={{32,0},{64,32},{96,64},{128,96},{160,128},{192,160},{224,192},{33,... | collective-permute-start | bytes 1228808 | tf_op jit(solution)/shard_map/ppermute | solution.py:10
  24.9 293.7 %copy-start.4 = (bf16[1,80,2560]{2,1,0:T(8,128)(2,1)S(1)}, bf16[1,80,2560]{2,1,0:T(8,128)(2,1)}, u32[]{:S(2)}) copy-start(bf16[1,80,2560]{2,1,0:T(8,128)(2,1)} %param.8) | copy-start | bytes 1228804
  24.9 293.7 %copy-start.6 = (bf16[1,80,2560]{2,1,0:T(8,128)(2,1)S(1)}, bf16[1,80,2560]{2,1,0:T(8,128)(2,1)}, u32[]{:S(2)}) copy-start(bf16[1,80,2560]{2,1,0:T(8,128)(2,1)} %param.6) | copy-start | bytes 1228804
  318.6 3.2 copy-start.5
  318.6 126.3 %copy-start.2 = (bf16[1,80,2560]{2,1,0:T(8,128)(2,1)S(1)}, bf16[1,80,2560]{2,1,0:T(8,128)(2,1)}, u32[]{:S(2)}) copy-start(bf16[1,80,2560]{2,1,0:T(8,128)(2,1)} %param.9) | copy-start | bytes 1228804
  321.8 134.9 %copy-start.3 = (bf16[1,80,2560]{2,1,0:T(8,128)(2,1)S(1)}, bf16[1,80,2560]{2,1,0:T(8,128)(2,1)}, u32[]{:S(2)}) copy-start(bf16[1,80,2560]{2,1,0:T(8,128)(2,1)} %param.7) | copy-start | bytes 1228804
  321.8 137.6 %collective-permute-start.2 = (bf16[20,128,128]{2,1,0:T(8,128)(2,1)S(1)}, bf16[20,128,128]{2,1,0:T(8,128)(2,1)S(1)}, u32[]{:S(2)}, u32[]{:S(2)}) collective-permute-start(bf16[20,128,128]{2,1,0:T(8,128)(2,1)S(1)} %bitcast.72), channel_id=1, source_target_pairs={{0,32},{32,64},{64,96},{96,128},{128,160},{160,192},{192,224},{1,3... | collective-permute-start | bytes 1966088 | tf_op jit(solution)/shard_map/ppermute | solution.py:10
  444.9 11.8 %copy-start.1 = (bf16[2560,2560]{1,0:T(8,128)(2,1)S(1)}, bf16[2560,2560]{1,0:T(8,128)(2,1)}, u32[]{:S(2)}) copy-start(bf16[2560,2560]{1,0:T(8,128)(2,1)} %all-gather.2.cloned.1.call-done) | copy-start | bytes 39321604
  452.6 8.9 %collective-permute-start.1 = (bf16[80,2560]{1,0:T(8,128)(2,1)S(1)}, bf16[80,2560]{1,0:T(8,128)(2,1)S(1)}, u32[]{:S(2)}, u32[]{:S(2)}) collective-permute-start(bf16[80,2560]{1,0:T(8,128)(2,1)S(1)} %bitcast.73), channel_id=1, source_target_pairs={{0,32},{32,64},{64,96},{96,128},{128,160},{160,192},{192,224},{1,3... | collective-permute-start | bytes 1228808 | tf_op jit(solution)/shard_map/ppermute | solution.py:10
Sparse Core Ops, SparseCore 0:
  321.9 122.9 all-gather.1
